TPU v7x, 256 devices: a whole 4x4x8 slice. The times are simulated.
256 devices in a mesh: row: 2 (over core), col: 128 (over z, y, x).
Axes of the slice: x: 4, y: 4, z: 8, core: 2. Of those that a mesh axis runs over, the one named last changes fastest.
Arguments:
- image_tokens: bfloat16 [64, 4096, 256], P('row', 'col'), may hold values from -6 to 6
- w_in: bfloat16 [256, 768], replicated, may hold values from -0.375 to 0.375
- conv_kernel: bfloat16 [3, 3, 768], replicated, may hold values from -2 to 2
- conv_bias: float32 [768], replicated, may hold values from -3 to 3
- long_filter: bfloat16 [64, 256], replicated, may hold values from -0.75 to 0.75
- skip_gain: float32 [256], replicated, may hold values from 0.5 to 1.5
- w_out: bfloat16 [256, 256], replicated, may hold values from -0.375 to 0.375
Outputs:
- layer_out: bfloat16 [64, 4096, 256], P('row', 'col')
All inputs are finite; a program needn't handle non-finite values.
Results may differ from a plain program's by a relative error of at most 0.014.
Values may be sent and summed in bfloat16 or wider, within the bound.
A program may use at most 64 MiB of HBM per device.

v0:
```python
import jax
import jax.numpy as jnp
from jax import lax
from jax.sharding import PartitionSpec as P


def extended(block, sides, width):
    for axis, dim in sides:
        count = lax.axis_size(axis)
        forward = [(i, i + 1) for i in range(count - 1)]
        backward = [(target, source) for source, target in forward]
        low = lax.ppermute(
            lax.slice_in_dim(block, block.shape[dim] - width, None, axis=dim), axis, forward
        )
        high = lax.ppermute(lax.slice_in_dim(block, 0, width, axis=dim), axis, backward)
        block = jnp.concatenate([low, block, high], axis=dim)
    return block


def depthwise(padded, kernel, bias, height, span):
    total = jnp.zeros((height, span, padded.shape[2]), jnp.float32) + bias
    for row_off in range(3):
        for col_off in range(3):
            window = padded[row_off : row_off + height, col_off : col_off + span, :].astype(
                jnp.float32
            )
            total = total + window * kernel[row_off, col_off].astype(jnp.float32)
    return total.astype(jnp.bfloat16)


def toeplitz(filt_rev, offset, out_count, src_count):
    margin = filt_rev.shape[0] // 3
    spare = margin // 2
    length = out_count + src_count - 1
    start = jnp.asarray(margin + margin - 1 - spare - (out_count - 1), jnp.int32) - jnp.asarray(
        offset, jnp.int32
    )
    window = lax.dynamic_slice_in_dim(filt_rev, start, length, 0)
    tiled = jnp.tile(window, (out_count + 1, 1))
    strided = tiled[out_count - 1 : out_count - 1 + out_count * (length - 1)]
    return strided.reshape(out_count, length - 1, filt_rev.shape[1])[:, :src_count]


def on_device(image_tokens, w_in, conv_kernel, conv_bias, long_filter, skip_gain, w_out):
    row_count, col_count, width = image_tokens.shape
    flat = image_tokens.reshape(row_count * col_count, width)
    projected = jnp.dot(flat, w_in, preferred_element_type=jnp.float32)
    projected = projected.astype(jnp.bfloat16).reshape(row_count, col_count, 3 * width)
    padded = extended(projected, (("row", 0), ("col", 1)), 1)
    mixed = depthwise(padded, conv_kernel, conv_bias, row_count, col_count)
    query = mixed[:, :, :width].astype(jnp.float32)
    key = mixed[:, :, width : 2 * width].astype(jnp.float32)
    value = mixed[:, :, 2 * width :].astype(jnp.float32)
    product = (key * value).astype(jnp.bfloat16)
    filt_pad = jnp.concatenate([jnp.zeros_like(long_filter), long_filter], axis=0)
    zero_band = jnp.zeros_like(filt_pad)
    filt_rev = jnp.concatenate([zero_band, jnp.flip(filt_pad, 0), zero_band], axis=0)
    my_start = lax.axis_index("row") * row_count
    empty_long = jnp.zeros((row_count, col_count, width), jnp.float32)
    total = empty_long
    piece = lax.all_gather(product, "row", axis=0, tiled=True)
    start = jnp.int32(0)
    piece_len = piece.shape[0]
    step_len = min(row_count, piece_len)
    for offset_row in range(0, piece_len, step_len):
        sub_piece = piece[offset_row : offset_row + step_len]
        sub_start = start + offset_row

        def work(running):
            toeplitz_block = toeplitz(filt_rev, my_start - sub_start, row_count, step_len)
            return running + jnp.einsum(
                "abc,bwc->awc", toeplitz_block, sub_piece, preferred_element_type=jnp.float32
            )

        def keep(running):
            return running

        total = lax.cond(sub_start < my_start + row_count, work, keep, total)
    gated = (query * (total + skip_gain * product.astype(jnp.float32))).astype(jnp.bfloat16)
    gated_flat = gated.reshape(row_count * col_count, width)
    final = jnp.dot(gated_flat, w_out, preferred_element_type=jnp.float32)
    return final.astype(jnp.bfloat16).reshape(row_count, col_count, width)


def solution(mesh):
    in_specs = (P("row", "col", None), P(), P(), P(), P(), P(), P())
    out_specs = P("row", "col", None)
    return jax.shard_map(
        on_device, mesh=mesh, in_specs=in_specs, out_specs=out_specs, check_vma=False
    )
```

profile of v0, /device:TPU:1, one launch (start us, length us, event | category | flops | bytes accessed | tf_op | source)
XLA Modules:
  0.0 115.1 jit_solution(9710104501801222011)
XLA Ops:
  7.6 1.6 %convolution_convert_fusion = bf16[1024,768]{1,0:T(8,128)(2,1)S(1)} fusion(bf16[1024,256]{1,0:T(8,128)(2,1)S(1)} %bitcast.18, bf16[256,768]{1,0:T(8,128)(2,1)} %param.12), kind=kOutput, calls=%fused_computation.9 | convolution fusion | flops 403439616 | bytes 2490368 | tf_op jit(solution)/shard_map/dot_general | solution.py:47
  9.2 1.3 %collective-permute-start = (bf16[1,32,768]{2,1,0:T(8,128)(2,1)S(1)}, bf16[1,32,768]{2,1,0:T(8,128)(2,1)S(1)}, u32[]{:S(2)}, u32[]{:S(2)}) collective-permute-start(bf16[1,32,768]{2,1,0:T(8,128)(2,1)S(1)} %get-tuple-element.63), channel_id=1, source_target_pairs={{0,128},{1,129},{2,130},{3,131},{4,132},{5,133},{6,134},{7,135},{8... | collective-permute-start | bytes 147464 | tf_op jit(solution)/shard_map/ppermute | solution.py:12
  10.5 5.1 %collective-permute-start.1 = (bf16[1,32,768]{2,1,0:T(8,128)(2,1)S(1)}, bf16[1,32,768]{2,1,0:T(8,128)(2,1)S(1)}, u32[]{:S(2)}, u32[]{:S(2)}) collective-permute-start(bf16[1,32,768]{2,1,0:T(8,128)(2,1)S(1)} %get-tuple-element.64), channel_id=1, source_target_pairs={{128,0},{129,1},{130,2},{131,3},{132,4},{133,5},{134,6},{135,7},{1... | collective-permute-start | bytes 147464 | tf_op jit(solution)/shard_map/ppermute | solution.py:15
  16.7 1.8 %collective-permute-start.2 = (bf16[34,1,768]{2,1,0:T(2,128)(2,1)S(1)}, bf16[34,1,768]{2,1,0:T(2,128)(2,1)S(1)}, u32[]{:S(2)}, u32[]{:S(2)}) collective-permute-start(bf16[34,1,768]{2,1,0:T(2,128)(2,1)S(1)} %get-tuple-element.61), channel_id=1, source_target_pairs={{0,1},{1,2},{2,3},{3,4},{4,5},{5,6},{6,7},{7,8},{8,9},{9,10},{10,1... | collective-permute-start | bytes 156680 | tf_op jit(solution)/shard_map/ppermute | solution.py:12
  20.4 3.8 %collective-permute-done.3 = bf16[34,1,768]{2,1,0:T(2,128)(2,1)S(1)} collective-permute-done((bf16[34,1,768]{2,1,0:T(2,128)(2,1)S(1)}, bf16[34,1,768]{2,1,0:T(2,128)(2,1)S(1)}, u32[]{:S(2)}, u32[]{:S(2)}) %collective-permute-start.3) | collective-permute-done | bytes 52256 | tf_op jit(solution)/shard_map/ppermute | solution.py:15
  25.5 4.1 %add_convert_fusion = bf16[32,32,768]{2,1,0:T(8,128)(2,1)S(1)} fusion(bf16[32,32,768]{2,1,0:T(8,128)(2,1)S(1)} %bitcast.21, bf16[34,33,768]{2,1,0:T(8,128)(2,1)S(1)} %get-tuple-element.60, bf16[1,32,768]{2,1,0:T(8,128)(2,1)S(1)} %collective-permute-done.1, bf16[34,33,768]{2,1,0:T(8,128)(2,1)S(1)} %get-tuple-element.59, ...), kind=kLoop, calls=%fused_computation.6 | loop fusion | flops 23592960 | bytes 12711936 | tf_op jit(solution)/shard_map/convert_element_type | solution.py:28
  30.7 22.5 %all-gather.2.cloned.1.call-done = bf16[64,32,256]{2,1,0:T(8,128)(2,1)} async-done(((bf16[32,32,256]{2,1,0:T(8,128)(2,1)}), bf16[64,32,256]{2,1,0:T(8,128)(2,1)}) %all-gather.2.cloned.1.call-update) | async-done | bytes 1048592 | tf_op jit(solution)/shard_map/all_gather | solution.py:61
  53.2 24.2 %conditional.2 = (f32[32,32,256]{1,0,2:T(8,128)}) conditional(s32[]{:T(128)} %convert_element_type.91, () %tuple.17, (s32[]{:T(128)}, bf16[384,256]{1,0:T(8,128)(2,1)S(1)}, bf16[64,32,256]{2,1,0:T(8,128)(2,1)}) %tuple.18), branch_computations={%region_0.1_spmd, %region_1.2_spmd} | conditional | flops 16777220 | bytes 20984918 | solution.py:78
  53.4 1.3 %tile.10 = bf16[2079,256]{1,0:T(8,128)(2,1)} reshape(bf16[33,63,256]{2,1,0:T(8,128)(2,1)S(1)} %tile.4) | data formatting | bytes 2128896 | tf_op jit(solution)/shard_map/cond/branch_1_fun/tile | solution.py:39
  54.7 2.5 %slice.133 = bf16[1984,256]{1,0:T(8,128)(2,1)} slice(bf16[2079,256]{1,0:T(8,128)(2,1)} %tile.10), slice={[31:2015], [0:256]} | slice | bytes 2031616 | tf_op jit(solution)/shard_map/cond/branch_1_fun/slice | solution.py:40
  57.2 2.3 %reshape.24 = bf16[32,62,256]{2,1,0:T(8,128)(2,1)} reshape(bf16[1984,256]{1,0:T(8,128)(2,1)} %slice.133) | data formatting | bytes 2031616 | tf_op jit(solution)/shard_map/cond/branch_1_fun/reshape | solution.py:41
  59.5 1.9 %slice.134 = bf16[32,32,256]{2,1,0:T(8,128)(2,1)} slice(bf16[32,62,256]{2,1,0:T(8,128)(2,1)} %reshape.24), slice={[0:32], [0:32], [0:256]} | slice | bytes 1048576 | tf_op jit(solution)/shard_map/cond/branch_1_fun/slice | solution.py:41
  61.4 4.6 %copy.29 = bf16[32,32,256]{1,0,2:T(8,128)(2,1)} copy(bf16[32,32,256]{2,1,0:T(8,128)(2,1)} %slice.134) | data formatting | bytes 1048576 | tf_op jit(solution)/shard_map/cond
  66.0 6.5 %copy.24 = bf16[64,32,256]{1,0,2:T(8,128)(2,1)} copy(bf16[64,32,256]{2,1,0:T(8,128)(2,1)S(1)} %copy-done.1) | data formatting | bytes 2097152 | tf_op jit(solution)/shard_map
  72.5 4.9 %convolution_bitcast_fusion = f32[32,32,256]{1,0,2:T(8,128)} fusion(bf16[32,32,256]{1,0,2:T(8,128)(2,1)} %copy.29, bf16[64,32,256]{1,0,2:T(8,128)(2,1)} %copy.24), kind=kOutput, calls=%fused_computation | convolution fusion | flops 16777216 | bytes 5242880 | tf_op jit(solution)/shard_map/cond/branch_1_fun/abc,bwc->awc/dot_general | solution.py:71
  77.4 28.8 %conditional.3 = (f32[32,32,256]{2,1,0:T(8,128)S(1)}) conditional(s32[]{:T(128)} %convert_element_type.90, f32[32,32,256]{1,0,2:T(8,128)} %get-tuple-element.67, (s32[]{:T(128)}, bf16[384,256]{1,0:T(8,128)(2,1)S(1)}, bf16[64,32,256]{2,1,0:T(8,128)(2,1)}, f32[32,32,256]{1,0,2:T(8,128)}) %tuple.19), branch_computations={%region_2.3_spmd, %region_3.4_spmd} | conditional | flops 17039364 | bytes 27276386 | solution.py:78
  77.6 1.3 %tile.12 = bf16[2079,256]{1,0:T(8,128)(2,1)} reshape(bf16[33,63,256]{2,1,0:T(8,128)(2,1)S(1)} %tile.11) | data formatting | bytes 2128896 | tf_op jit(solution)/shard_map/cond/branch_1_fun/tile | solution.py:39
  78.9 2.4 %slice.136 = bf16[1984,256]{1,0:T(8,128)(2,1)} slice(bf16[2079,256]{1,0:T(8,128)(2,1)} %tile.12), slice={[31:2015], [0:256]} | slice | bytes 2031616 | tf_op jit(solution)/shard_map/cond/branch_1_fun/slice | solution.py:40
  81.3 2.4 %reshape.25 = bf16[32,62,256]{2,1,0:T(8,128)(2,1)} reshape(bf16[1984,256]{1,0:T(8,128)(2,1)} %slice.136) | data formatting | bytes 2031616 | tf_op jit(solution)/shard_map/cond/branch_1_fun/reshape | solution.py:41
  83.7 1.9 %slice.137 = bf16[32,32,256]{2,1,0:T(8,128)(2,1)} slice(bf16[32,62,256]{2,1,0:T(8,128)(2,1)} %reshape.25), slice={[0:32], [0:32], [0:256]} | slice | bytes 1048576 | tf_op jit(solution)/shard_map/cond/branch_1_fun/slice | solution.py:41
  85.5 4.6 %copy.30 = bf16[32,32,256]{1,0,2:T(8,128)(2,1)} copy(bf16[32,32,256]{2,1,0:T(8,128)(2,1)} %slice.137) | data formatting | bytes 1048576 | tf_op jit(solution)/shard_map/cond
  90.1 6.5 %copy.25 = bf16[64,32,256]{1,0,2:T(8,128)(2,1)} copy(bf16[64,32,256]{2,1,0:T(8,128)(2,1)S(1)} %copy-done.2) | data formatting | bytes 2097152 | tf_op jit(solution)/shard_map
  96.6 6.1 %bitcast_add_fusion = f32[32,32,256]{1,0,2:T(8,128)} fusion(f32[32,32,256]{1,0,2:T(8,128)} %get-tuple-element.30, bf16[32,32,256]{1,0,2:T(8,128)(2,1)} %copy.30, bf16[64,32,256]{1,0,2:T(8,128)(2,1)} %copy.25), kind=kOutput, calls=%fused_computation.3 | convolution fusion | flops 17039360 | bytes 9437184 | tf_op jit(solution)/shard_map/cond/branch_1_fun/abc,bwc->awc/dot_general | solution.py:71
  102.7 3.5 %copy.28 = f32[32,32,256]{2,1,0:T(8,128)S(1)} copy(f32[32,32,256]{1,0,2:T(8,128)} %bitcast_add_fusion) | data formatting | bytes 2097152 | tf_op jit(solution)/shard_map/cond | solution.py:78
  (37 shorter events, 8.6 us)
Async XLA Ops:
  6.5 1.0 copy-start
  6.5 13.3 %copy-start.4 = (bf16[3,3,768]{2,1,0:T(4,128)(2,1)S(1)}, bf16[3,3,768]{2,1,0:T(4,128)(2,1)}, u32[]{:S(2)}) copy-start(bf16[3,3,768]{2,1,0:T(4,128)(2,1)} %param.13) | copy-start | bytes 41476
  6.5 46.7 %all-gather.2.cloned.1.call-start = ((), (), s32[]{:S(2)}) async-start(), calls=%async_computation | async-start | bytes 1572864 | tf_op jit(solution)/shard_map/all_gather | solution.py:61
  9.2 6.5 %collective-permute-start = (bf16[1,32,768]{2,1,0:T(8,128)(2,1)S(1)}, bf16[1,32,768]{2,1,0:T(8,128)(2,1)S(1)}, u32[]{:S(2)}, u32[]{:S(2)}) collective-permute-start(bf16[1,32,768]{2,1,0:T(8,128)(2,1)S(1)} %get-tuple-element.63), channel_id=1, source_target_pairs={{0,128},{1,129},{2,130},{3,131},{4,132},{5,133},{6,134},{7,135},{8... | collective-permute-start | bytes 147464 | tf_op jit(solution)/shard_map/ppermute | solution.py:12
  10.5 6.0 %collective-permute-start.1 = (bf16[1,32,768]{2,1,0:T(8,128)(2,1)S(1)}, bf16[1,32,768]{2,1,0:T(8,128)(2,1)S(1)}, u32[]{:S(2)}, u32[]{:S(2)}) collective-permute-start(bf16[1,32,768]{2,1,0:T(8,128)(2,1)S(1)} %get-tuple-element.64), channel_id=1, source_target_pairs={{128,0},{129,1},{130,2},{131,3},{132,4},{133,5},{134,6},{135,7},{1... | collective-permute-start | bytes 147464 | tf_op jit(solution)/shard_map/ppermute | solution.py:15
  16.6 8.8 %copy-start.6 = (f32[768]{0:T(1024)S(1)}, f32[768]{0:T(1024)}, u32[]{:S(2)}) copy-start(f32[768]{0:T(1024)} %param.14) | copy-start | bytes 9220
  16.7 3.8 %collective-permute-start.2 = (bf16[34,1,768]{2,1,0:T(2,128)(2,1)S(1)}, bf16[34,1,768]{2,1,0:T(2,128)(2,1)S(1)}, u32[]{:S(2)}, u32[]{:S(2)}) collective-permute-start(bf16[34,1,768]{2,1,0:T(2,128)(2,1)S(1)} %get-tuple-element.61), channel_id=1, source_target_pairs={{0,1},{1,2},{2,3},{3,4},{4,5},{5,6},{6,7},{7,8},{8,9},{9,10},{10,1... | collective-permute-start | bytes 156680 | tf_op jit(solution)/shard_map/ppermute | solution.py:12
  18.5 5.7 %collective-permute-start.3 = (bf16[34,1,768]{2,1,0:T(2,128)(2,1)S(1)}, bf16[34,1,768]{2,1,0:T(2,128)(2,1)S(1)}, u32[]{:S(2)}, u32[]{:S(2)}) collective-permute-start(bf16[34,1,768]{2,1,0:T(2,128)(2,1)S(1)} %get-tuple-element.62), channel_id=1, source_target_pairs={{1,0},{2,1},{3,2},{4,3},{5,4},{6,5},{7,6},{8,7},{9,8},{10,9},{11,1... | collective-permute-start | bytes 156680 | tf_op jit(solution)/shard_map/ppermute | solution.py:15
  25.5 5.1 %copy-start.5 = (bf16[64,256]{1,0:T(8,128)(2,1)S(1)}, bf16[64,256]{1,0:T(8,128)(2,1)}, u32[]{:S(2)}) copy-start(bf16[64,256]{1,0:T(8,128)(2,1)} %param.15) | copy-start | bytes 98308
  57.2 8.8 %copy-start.1 = (bf16[64,32,256]{2,1,0:T(8,128)(2,1)S(1)}, bf16[64,32,256]{2,1,0:T(8,128)(2,1)}, u32[]{:S(2)}) copy-start(bf16[64,32,256]{2,1,0:T(8,128)(2,1)} %get-tuple-element.44) | copy-start | bytes 3145732 | tf_op jit(solution)/shard_map/cond
  77.4 28.8 %copy-start.7 = (f32[256]{0:T(256)S(1)}, f32[256]{0:T(256)}, u32[]{:S(2)}) copy-start(f32[256]{0:T(256)} %param.16) | copy-start | bytes 3076
  81.3 8.8 %copy-start.2 = (bf16[64,32,256]{2,1,0:T(8,128)(2,1)S(1)}, bf16[64,32,256]{2,1,0:T(8,128)(2,1)}, u32[]{:S(2)}) copy-start(bf16[64,32,256]{2,1,0:T(8,128)(2,1)} %get-tuple-element.47) | copy-start | bytes 3145732 | tf_op jit(solution)/shard_map/cond
  106.2 0.9 copy-start.3
Sparse Core Ops, SparseCore 0:
  30.7 22.5 all-gather.1
where the time goes:
time: 116 us; the launch traced here: 115 us
  local copies, waits for them, and re-layouts  43.7 us (38%)
  waiting for transfers between devices  27.7 us (24%)
  matrix products  13.7 us (12%)
  between operations  13.6 us (12%)
  starting transfers between devices  9.57 us (8%)
  other arithmetic  6.79 us (6%)
    all_gather x1, waiting for transfers between devices, on_device(): piece = lax.all_gather(product, 'row', axis=0, tiled=True)  22.5 us
    another operation x2, local copies, waits for them, and re-layouts  13 us
    dot_general x2, matrix products, work(): jnp.einsum('abc,bwc->awc', toeplitz_block, sub_piece, preferred_element_t...  11.1 us
    cond x6, local copies, waits for them, and re-layouts  9.15 us
    ppermute x2, starting transfers between devices, extended(): lax.ppermute(lax.slice_in_dim(block, 0, width, axis=dim), axis, backward)  6.44 us
    slice x2, local copies, waits for them, and re-layouts, toeplitz(): strided = tiled[out_count - 1:out_count - 1 + out_count * (length - 1)]  4.91 us
    reshape x2, local copies, waits for them, and re-layouts, toeplitz(): strided.reshape(out_count, length - 1, filt_rev.shape[1])[:, :src_count]  4.73 us
    ppermute x2, waiting for transfers between devices, extended(): lax.ppermute(lax.slice_in_dim(block, 0, width, axis=dim), axis, backward)  4.65 us
  transfers between devices with their start and end apart: 5, of which 4 were waited for; matrix products, arithmetic and copies ran while one was open for 0% of the time, Pallas kernels for 0%

commit v1 on v0

--- a/solution.py
+++ b/solution.py
@@ -2,6 +2,7 @@
 import jax.numpy as jnp
 from jax import lax
 from jax.sharding import PartitionSpec as P
+from jax.lax import all_to_all, axis_size
 
 
 def extended(block, sides, width):
@@ -58,7 +59,10 @@
     my_start = lax.axis_index("row") * row_count
     empty_long = jnp.zeros((row_count, col_count, width), jnp.float32)
     total = empty_long
-    piece = lax.all_gather(product, "row", axis=0, tiled=True)
+    start_task = lambda xs: jnp.concatenate(
+        all_to_all(jnp.stack([xs for _ in range(axis_size("row"))], axis=0), "row", 0, 0), axis=0
+    )
+    piece = start_task(product)
     start = jnp.int32(0)
     piece_len = piece.shape[0]
     step_len = min(row_count, piece_len)

time: 116 us -> 89.8 us (0.77)
  the two profiles are of different devices: /device:TPU:1 before, /device:TPU:127 now
where the time goes in v1:
time: 89.8 us; the launch traced here: 89.2 us
  local copies, waits for them, and re-layouts  43.8 us (49%)
  matrix products  13.6 us (15%)
  starting transfers between devices  10.6 us (12%)
  waiting for transfers between devices  9.22 us (10%)
  other arithmetic  6.09 us (7%)
  blocking collectives  5.61 us (6%)
    another operation x2, local copies, waits for them, and re-layouts  12.9 us
    dot_general x2, matrix products, work(): jnp.einsum('abc,bwc->awc', toeplitz_block, sub_piece, preferred_element_t...  11 us
    ppermute x2, waiting for transfers between devices, extended(): lax.ppermute(lax.slice_in_dim(block, 0, width, axis=dim), axis, backward)  9.21 us
    cond x2, local copies, waits for them, and re-layouts  8.31 us
    ppermute x2, starting transfers between devices, extended(): lax.ppermute(lax.slice_in_dim(block, block.shape[dim] - width, None, axis...  5.62 us
    all_to_all x1, blocking collectives, on_device(): all_to_all(jnp.stack([xs for _ in range(axis_size('row'))], axis=0), 'row...  5.61 us
    another operation x4, local copies, waits for them, and re-layouts, toeplitz(): tiled = jnp.tile(window, (out_count + 1, 1))  4.96 us
    ppermute x2, starting transfers between devices, extended(): lax.ppermute(lax.slice_in_dim(block, 0, width, axis=dim), axis, backward)  4.95 us
  transfers between devices with their start and end apart: 4, of which 1 were waited for; matrix products, arithmetic and copies ran while one was open for 1% of the time, Pallas kernels for 0%

profile of v1, /device:TPU:127, one launch (start us, length us, event | category | flops | bytes accessed | tf_op | source)
XLA Modules:
  0.0 89.2 jit_solution(1491118594156590473)
XLA Ops:
  1.0 1.6 %convolution_convert_fusion = bf16[1024,768]{1,0:T(8,128)(2,1)S(1)} fusion(bf16[1024,256]{1,0:T(8,128)(2,1)S(1)} %bitcast.26, bf16[256,768]{1,0:T(8,128)(2,1)} %param.12), kind=kOutput, calls=%fused_computation.9 | convolution fusion | flops 403439616 | bytes 2490368 | tf_op jit(solution)/shard_map/dot_general | solution.py:48
  2.6 1.3 %collective-permute-start = (bf16[1,32,768]{2,1,0:T(8,128)(2,1)S(1)}, bf16[1,32,768]{2,1,0:T(8,128)(2,1)S(1)}, u32[]{:S(2)}, u32[]{:S(2)}) collective-permute-start(bf16[1,32,768]{2,1,0:T(8,128)(2,1)S(1)} %get-tuple-element.58), channel_id=1, source_target_pairs={{0,128},{1,129},{2,130},{3,131},{4,132},{5,133},{6,134},{7,135},{8... | collective-permute-start | bytes 147464 | tf_op jit(solution)/shard_map/ppermute | solution.py:13
  3.9 3.0 %collective-permute-start.1 = (bf16[1,32,768]{2,1,0:T(8,128)(2,1)S(1)}, bf16[1,32,768]{2,1,0:T(8,128)(2,1)S(1)}, u32[]{:S(2)}, u32[]{:S(2)}) collective-permute-start(bf16[1,32,768]{2,1,0:T(8,128)(2,1)S(1)} %get-tuple-element.59), channel_id=1, source_target_pairs={{128,0},{129,1},{130,2},{131,3},{132,4},{133,5},{134,6},{135,7},{1... | collective-permute-start | bytes 147464 | tf_op jit(solution)/shard_map/ppermute | solution.py:16
  8.1 4.3 %collective-permute-start.2 = (bf16[34,1,768]{2,1,0:T(2,128)(2,1)S(1)}, bf16[34,1,768]{2,1,0:T(2,128)(2,1)S(1)}, u32[]{:S(2)}, u32[]{:S(2)}) collective-permute-start(bf16[34,1,768]{2,1,0:T(2,128)(2,1)S(1)} %get-tuple-element.56), channel_id=1, source_target_pairs={{0,1},{1,2},{2,3},{3,4},{4,5},{5,6},{6,7},{7,8},{8,9},{9,10},{10,1... | collective-permute-start | bytes 156680 | tf_op jit(solution)/shard_map/ppermute | solution.py:13
  12.4 1.9 %collective-permute-start.3 = (bf16[34,1,768]{2,1,0:T(2,128)(2,1)S(1)}, bf16[34,1,768]{2,1,0:T(2,128)(2,1)S(1)}, u32[]{:S(2)}, u32[]{:S(2)}) collective-permute-start(bf16[34,1,768]{2,1,0:T(2,128)(2,1)S(1)} %get-tuple-element.57), channel_id=1, source_target_pairs={{1,0},{2,1},{3,2},{4,3},{5,4},{6,5},{7,6},{8,7},{9,8},{10,9},{11,1... | collective-permute-start | bytes 156680 | tf_op jit(solution)/shard_map/ppermute | solution.py:16
  14.5 9.2 %collective-permute-done.3 = bf16[34,1,768]{2,1,0:T(2,128)(2,1)S(1)} collective-permute-done((bf16[34,1,768]{2,1,0:T(2,128)(2,1)S(1)}, bf16[34,1,768]{2,1,0:T(2,128)(2,1)S(1)}, u32[]{:S(2)}, u32[]{:S(2)}) %collective-permute-start.3) | collective-permute-done | bytes 52256 | tf_op jit(solution)/shard_map/ppermute | solution.py:16
  24.9 4.1 %add_convert_fusion = bf16[32,32,768]{2,1,0:T(8,128)(2,1)S(1)} fusion(bf16[32,32,768]{2,1,0:T(8,128)(2,1)S(1)} %bitcast.29, bf16[34,33,768]{2,1,0:T(8,128)(2,1)S(1)} %get-tuple-element.55, bf16[1,32,768]{2,1,0:T(8,128)(2,1)S(1)} %collective-permute-done.1, bf16[34,33,768]{2,1,0:T(8,128)(2,1)S(1)} %get-tuple-element.54, ...), kind=kLoop, calls=%fused_computation.6 | loop fusion | flops 23592960 | bytes 12711936 | tf_op jit(solution)/shard_map/convert_element_type | solution.py:29
  30.4 5.6 %all_to_all.5 = bf16[2,32,32,256]{3,2,1,0:T(8,128)(2,1)S(1)} all-to-all(bf16[2,32,32,256]{3,2,1,0:T(8,128)(2,1)S(1)} %pad_maximum_fusion.3), channel_id=1, replica_groups=mesh['row'=2,'col'=128] {'row'}, dimensions={0} | all-to-all | bytes 2097152 | tf_op jit(solution)/shard_map/all_to_all | solution.py:63
  36.1 20.3 %conditional.2 = (f32[32,32,256]{1,0,2:T(8,128)}) conditional(s32[]{:T(128)} %convert_element_type.91, () %tuple.17, (s32[]{:T(128)}, bf16[384,256]{1,0:T(8,128)(2,1)S(1)}, bf16[2,32,32,256]{3,2,1,0:T(8,128)(2,1)S(1)}) %tuple.18), branch_computations={%region_0.1_spmd, %region_1.2_spmd} | conditional | flops 16777220 | bytes 16790586 | solution.py:82
  36.2 1.3 %tile.10 = bf16[2079,256]{1,0:T(8,128)(2,1)} reshape(bf16[33,63,256]{2,1,0:T(8,128)(2,1)S(1)} %tile.4) | data formatting | bytes 2128896 | tf_op jit(solution)/shard_map/cond/branch_1_fun/tile | solution.py:40
  37.5 1.5 %slice.141 = bf16[1984,256]{1,0:T(8,128)(2,1)S(1)} slice(bf16[2079,256]{1,0:T(8,128)(2,1)} %tile.10), slice={[31:2015], [0:256]} | slice | bytes 2031616 | tf_op jit(solution)/shard_map/cond/branch_1_fun/slice | solution.py:41
  39.0 1.3 %reshape.28 = bf16[32,62,256]{2,1,0:T(8,128)(2,1)} reshape(bf16[1984,256]{1,0:T(8,128)(2,1)S(1)} %slice.141) | data formatting | bytes 2031616 | tf_op jit(solution)/shard_map/cond/branch_1_fun/reshape | solution.py:42
  41.3 3.8 %copy.24 = bf16[32,32,256]{1,0,2:T(8,128)(2,1)} copy(bf16[32,32,256]{2,1,0:T(8,128)(2,1)S(1)} %slice.142) | data formatting | bytes 1048576 | tf_op jit(solution)/shard_map/cond
  45.1 6.4 %copy.19 = bf16[2,32,32,256]{2,1,3,0:T(8,128)(2,1)} copy(bf16[2,32,32,256]{3,2,1,0:T(8,128)(2,1)S(1)} %get-tuple-element.39) | data formatting | bytes 2097152 | tf_op jit(solution)/shard_map
  51.5 4.9 %convolution_bitcast_fusion = f32[32,32,256]{1,0,2:T(8,128)} fusion(bf16[32,32,256]{1,0,2:T(8,128)(2,1)} %copy.24, bf16[2,32,32,256]{2,1,3,0:T(8,128)(2,1)} %copy.19), kind=kOutput, calls=%fused_computation | convolution fusion | flops 16777216 | bytes 5242880 | tf_op jit(solution)/shard_map/cond/branch_1_fun/abc,bwc->awc/dot_general | solution.py:75
  56.4 30.8 %conditional.3 = (f32[32,32,256]{2,1,0:T(8,128)S(1)}) conditional(s32[]{:T(128)} %convert_element_type.90, f32[32,32,256]{1,0,2:T(8,128)} %get-tuple-element.62, (s32[]{:T(128)}, bf16[384,256]{1,0:T(8,128)(2,1)S(1)}, bf16[2,32,32,256]{3,2,1,0:T(8,128)(2,1)S(1)}, f32[32,32,256]{1,0,2:T(8,128)}) %tuple.19), branch_computations={%region_2.3_spmd, %region_3.4_spmd} | conditional | flops 17039364 | bytes 23082054 | solution.py:82
  57.6 2.4 %tile.12 = bf16[2079,256]{1,0:T(8,128)(2,1)} reshape(bf16[33,63,256]{2,1,0:T(8,128)(2,1)} %tile.11) | data formatting | bytes 2128896 | tf_op jit(solution)/shard_map/cond/branch_1_fun/tile | solution.py:40
  60.0 2.4 %slice.144 = bf16[1984,256]{1,0:T(8,128)(2,1)} slice(bf16[2079,256]{1,0:T(8,128)(2,1)} %tile.12), slice={[31:2015], [0:256]} | slice | bytes 2031616 | tf_op jit(solution)/shard_map/cond/branch_1_fun/slice | solution.py:41
  62.4 2.3 %reshape.29 = bf16[32,62,256]{2,1,0:T(8,128)(2,1)} reshape(bf16[1984,256]{1,0:T(8,128)(2,1)} %slice.144) | data formatting | bytes 2031616 | tf_op jit(solution)/shard_map/cond/branch_1_fun/reshape | solution.py:42
  64.7 1.9 %slice.145 = bf16[32,32,256]{2,1,0:T(8,128)(2,1)} slice(bf16[32,62,256]{2,1,0:T(8,128)(2,1)} %reshape.29), slice={[0:32], [0:32], [0:256]} | slice | bytes 1048576 | tf_op jit(solution)/shard_map/cond/branch_1_fun/slice | solution.py:42
  66.6 4.6 %copy.25 = bf16[32,32,256]{1,0,2:T(8,128)(2,1)} copy(bf16[32,32,256]{2,1,0:T(8,128)(2,1)} %slice.145) | data formatting | bytes 1048576 | tf_op jit(solution)/shard_map/cond
  71.1 6.4 %copy.20 = bf16[2,32,32,256]{2,1,3,0:T(8,128)(2,1)} copy(bf16[2,32,32,256]{3,2,1,0:T(8,128)(2,1)S(1)} %get-tuple-element.42) | data formatting | bytes 2097152 | tf_op jit(solution)/shard_map
  77.6 6.1 %bitcast_add_fusion = f32[32,32,256]{1,0,2:T(8,128)} fusion(f32[32,32,256]{1,0,2:T(8,128)} %get-tuple-element.31, bf16[32,32,256]{1,0,2:T(8,128)(2,1)} %copy.25, bf16[2,32,32,256]{2,1,3,0:T(8,128)(2,1)} %copy.20), kind=kOutput, calls=%fused_computation.3 | convolution fusion | flops 17039360 | bytes 9437184 | tf_op jit(solution)/shard_map/cond/branch_1_fun/abc,bwc->awc/dot_general | solution.py:75
  83.7 3.5 %copy.23 = f32[32,32,256]{2,1,0:T(8,128)S(1)} copy(f32[32,32,256]{1,0,2:T(8,128)} %bitcast_add_fusion) | data formatting | bytes 2097152 | tf_op jit(solution)/shard_map/cond | solution.py:82
  (34 shorter events, 9.2 us)
Async XLA Ops:
  0.0 1.0 %copy-start = (bf16[32,32,256]{2,1,0:T(8,128)(2,1)S(1)}, bf16[32,32,256]{2,1,0:T(8,128)(2,1)}, u32[]{:S(2)}) copy-start(bf16[32,32,256]{2,1,0:T(8,128)(2,1)} %param.11) | copy-start | bytes 1572868
  0.0 14.3 %copy-start.4 = (bf16[3,3,768]{2,1,0:T(4,128)(2,1)S(1)}, bf16[3,3,768]{2,1,0:T(4,128)(2,1)}, u32[]{:S(2)}) copy-start(bf16[3,3,768]{2,1,0:T(4,128)(2,1)} %param.13) | copy-start | bytes 41476
  2.6 5.3 %collective-permute-start = (bf16[1,32,768]{2,1,0:T(8,128)(2,1)S(1)}, bf16[1,32,768]{2,1,0:T(8,128)(2,1)S(1)}, u32[]{:S(2)}, u32[]{:S(2)}) collective-permute-start(bf16[1,32,768]{2,1,0:T(8,128)(2,1)S(1)} %get-tuple-element.58), channel_id=1, source_target_pairs={{0,128},{1,129},{2,130},{3,131},{4,132},{5,133},{6,134},{7,135},{8... | collective-permute-start | bytes 147464 | tf_op jit(solution)/shard_map/ppermute | solution.py:13
  3.9 4.0 %collective-permute-start.1 = (bf16[1,32,768]{2,1,0:T(8,128)(2,1)S(1)}, bf16[1,32,768]{2,1,0:T(8,128)(2,1)S(1)}, u32[]{:S(2)}, u32[]{:S(2)}) collective-permute-start(bf16[1,32,768]{2,1,0:T(8,128)(2,1)S(1)} %get-tuple-element.59), channel_id=1, source_target_pairs={{128,0},{129,1},{130,2},{131,3},{132,4},{133,5},{134,6},{135,7},{1... | collective-permute-start | bytes 147464 | tf_op jit(solution)/shard_map/ppermute | solution.py:16
  8.1 16.8 %copy-start.5 = (f32[768]{0:T(1024)S(1)}, f32[768]{0:T(1024)}, u32[]{:S(2)}) copy-start(f32[768]{0:T(1024)} %param.14) | copy-start | bytes 9220
  8.1 6.4 %collective-permute-start.2 = (bf16[34,1,768]{2,1,0:T(2,128)(2,1)S(1)}, bf16[34,1,768]{2,1,0:T(2,128)(2,1)S(1)}, u32[]{:S(2)}, u32[]{:S(2)}) collective-permute-start(bf16[34,1,768]{2,1,0:T(2,128)(2,1)S(1)} %get-tuple-element.56), channel_id=1, source_target_pairs={{0,1},{1,2},{2,3},{3,4},{4,5},{5,6},{6,7},{7,8},{8,9},{9,10},{10,1... | collective-permute-start | bytes 156680 | tf_op jit(solution)/shard_map/ppermute | solution.py:13
  12.4 11.3 %collective-permute-start.3 = (bf16[34,1,768]{2,1,0:T(2,128)(2,1)S(1)}, bf16[34,1,768]{2,1,0:T(2,128)(2,1)S(1)}, u32[]{:S(2)}, u32[]{:S(2)}) collective-permute-start(bf16[34,1,768]{2,1,0:T(2,128)(2,1)S(1)} %get-tuple-element.57), channel_id=1, source_target_pairs={{1,0},{2,1},{3,2},{4,3},{5,4},{6,5},{7,6},{8,7},{9,8},{10,9},{11,1... | collective-permute-start | bytes 156680 | tf_op jit(solution)/shard_map/ppermute | solution.py:16
  29.0 1.2 %copy-start.1 = (bf16[32,32,768]{2,1,0:T(8,128)(2,1)}, bf16[32,32,768]{2,1,0:T(8,128)(2,1)S(1)}, u32[]{:S(2)}) copy-start(bf16[32,32,768]{2,1,0:T(8,128)(2,1)S(1)} %add_convert_fusion) | copy-start | bytes 4718596
  56.4 30.8 %copy-start.2 = (bf16[32,32,768]{2,1,0:T(8,128)(2,1)S(1)}, bf16[32,32,768]{2,1,0:T(8,128)(2,1)}, u32[]{:S(2)}) copy-start(bf16[32,32,768]{2,1,0:T(8,128)(2,1)} %copy-done.1) | copy-start | bytes 4718596
  56.4 30.8 %copy-start.6 = (f32[256]{0:T(256)S(1)}, f32[256]{0:T(256)}, u32[]{:S(2)}) copy-start(f32[256]{0:T(256)} %param.16) | copy-start | bytes 3076
  87.2 0.9 %copy-start.3 = (bf16[256,256]{1,0:T(8,128)(2,1)S(1)}, bf16[256,256]{1,0:T(8,128)(2,1)}, u32[]{:S(2)}) copy-start(bf16[256,256]{1,0:T(8,128)(2,1)} %param.17) | copy-start | bytes 393220
